TPU v7x, 256 devices: a whole 4x4x8 slice. The times are simulated.
256 devices in a mesh: ta: 4 (over y), ha: 16 (over x, z_hi, core), wa: 4 (over z_lo).
Axes of the slice: x: 4, y: 4, z: 8 (z_hi: 2, z_lo: 4; z = z_hi * 4 + z_lo), core: 2. Of those that a mesh axis runs over, the one named last changes fastest.
Arguments:
- latents: bfloat16 [8, 256, 128, 256], P('ta', 'ha', 'wa'), may hold values from -6 to 6
- norm_gain: float32 [256], replicated, may hold values from 0.1 to 1.9
- conv_weight: bfloat16 [3, 3, 3, 256, 256], replicated, may hold values from -0.078125 to 0.078125
- qkv_weight: bfloat16 [1024, 16, 3, 128], P(None, ('ta', 'wa')), may hold values from -2.7 to 2.7
Outputs:
- block_out: bfloat16 [8, 256, 128, 256], P('ta', 'ha', 'wa')
- attended: bfloat16 [8, 128, 64, 16, 128], P(None, 'ha', None, ('ta', 'wa'))
All inputs are finite; a program needn't handle non-finite values.
Results may differ from a plain program's by a relative error of at most 0.0062.
Values may be sent and summed in bfloat16 or wider, within the bound.
No kernel may reach another device: no remote copies, remote signals or barrier semaphores. Data moves between devices by JAX's collectives and lax.ppermute only.
A program may use at most 128 MiB of HBM per device.

v0:
```python
import jax
import jax.numpy as jnp
from jax import lax
from jax.sharding import PartitionSpec as P

WIN = 4


def extended(cells, sides, width):
    for axis, dim in sides:
        count = lax.axis_size(axis)
        ends = count - 1
        head = lax.slice_in_dim(cells, 0, width, axis=dim)
        tail = lax.slice_in_dim(cells, cells.shape[dim] - width, cells.shape[dim], axis=dim)
        cells = jnp.concatenate(
            [
                lax.ppermute(tail, axis, [(i, (i + 1) % count) for i in range(ends)]),
                cells,
                lax.ppermute(head, axis, [((i + 1) % count, i) for i in range(ends)]),
            ],
            axis=dim,
        )
    return cells


def local(latents, norm_gain, conv_weight, qkv_weight):
    t_dev, h_dev, w_dev, channels = latents.shape
    rows_dev = h_dev // 2
    cols_dev = w_dev // 2
    latent_f32 = latents.astype(jnp.float32)
    scale_rms = lax.rsqrt(jnp.mean(latent_f32 * latent_f32, axis=-1, keepdims=True) + 1e-06)
    normed = jax.nn.silu(latent_f32 * scale_rms * norm_gain).astype(jnp.bfloat16)
    padded = extended(normed, (("ta", 0), ("ha", 1), ("wa", 2)), 1)
    conv_out = lax.conv_general_dilated(
        padded[None],
        conv_weight,
        (1, 1, 1),
        "VALID",
        dimension_numbers=("NDHWC", "DHWIO", "NDHWC"),
        preferred_element_type=jnp.float32,
    )[0]
    block_out = (latent_f32 + conv_out).astype(jnp.bfloat16)
    patches = (
        block_out.reshape(t_dev, rows_dev, 2, cols_dev, 2, channels)
        .transpose(0, 1, 3, 2, 4, 5)
        .reshape(t_dev * rows_dev * cols_dev, 4 * channels)
    )
    width_in, head_dev, qkv_count, head_size = qkv_weight.shape
    every_head = lax.all_gather(qkv_weight, ("ta", "wa"), axis=1, tiled=True)
    projected = jnp.dot(
        patches, every_head.reshape(width_in, -1), preferred_element_type=jnp.float32
    ).astype(jnp.bfloat16)
    gathered = lax.all_to_all(projected, ("ta", "wa"), split_axis=1, concat_axis=0, tiled=True)
    n_time = lax.axis_size("ta")
    n_width = lax.axis_size("wa")
    frames = n_time * t_dev
    patch_cols = n_width * cols_dev
    qkv_rows = gathered.reshape(
        n_time, n_width, t_dev, rows_dev, cols_dev, head_dev, qkv_count, head_size
    )
    qkv_rows = qkv_rows.transpose(0, 2, 3, 1, 4, 5, 6, 7).reshape(
        frames, rows_dev, patch_cols, head_dev, qkv_count, head_size
    )
    queries = qkv_rows[:, :, :, :, 0, :]
    key_value = qkv_rows[:, :, :, :, 1:, :].reshape(
        frames, rows_dev, patch_cols, head_dev, 2 * head_size
    )
    kv_rim = extended(key_value, (("ha", 1),), WIN)
    row_base = lax.axis_index("ha") * rows_dev
    total_rows = rows_dev * lax.axis_size("ha")

    def attend(block_idx):
        q_block = lax.dynamic_slice_in_dim(queries, block_idx * WIN, WIN, 1)
        kv_block = lax.dynamic_slice_in_dim(kv_rim, block_idx * WIN, 3 * WIN, 1)
        key_part = kv_block[..., :head_size]
        value_part = kv_block[..., head_size:]
        scores = jnp.einsum(
            "tiahd,tjbhd->thiajb", q_block, key_part, preferred_element_type=jnp.float32
        ) * head_size ** (-0.5)
        q_row = jnp.arange(WIN, dtype=jnp.int32)[:, None]
        k_row = jnp.arange(3 * WIN, dtype=jnp.int32)[None, :] - WIN
        k_global = row_base + block_idx * WIN + k_row
        allowed = (jnp.abs(q_row - k_row) <= WIN) & (k_global >= 0) & (k_global < total_rows)
        scores = jnp.where(allowed[None, None, :, None, :, None], scores, -1e30)
        row_max = jnp.max(scores, axis=(4, 5), keepdims=True)
        exp_scores = jnp.exp(scores - row_max)
        probs = (exp_scores / jnp.sum(exp_scores, axis=(4, 5), keepdims=True)).astype(jnp.bfloat16)
        result = jnp.einsum(
            "thiajb,tjbhd->tiahd", probs, value_part, preferred_element_type=jnp.float32
        )
        return result.astype(jnp.bfloat16)

    blocks = lax.map(attend, jnp.arange(rows_dev // WIN, dtype=jnp.int32))
    attended = blocks.transpose(1, 0, 2, 3, 4, 5).reshape(
        frames, rows_dev, patch_cols, head_dev, head_size
    )
    return (block_out, attended)


def solution(mesh):
    return jax.shard_map(
        local,
        mesh=mesh,
        in_specs=(P("ta", "ha", "wa", None), P(), P(), P(None, ("ta", "wa"), None, None)),
        out_specs=(P("ta", "ha", "wa", None), P(None, "ha", None, ("ta", "wa"), None)),
        check_vma=False,
    )
```

profile of v0, /device:TPU:3, one launch (start us, length us, event | category | flops | bytes accessed | tf_op | source)
XLA Modules:
  0.0 499.1 jit_solution(14405158100643521824)
XLA Ops:
  7.2 0.7 all-gather.2.cloned.1.call-update
  7.9 1.7 fusion.27
  9.7 1.5 fusion.34
  11.2 3.2 collective-permute-start
  14.5 1.3 collective-permute-start.1
  15.8 3.7 collective-permute-done
  19.4 3.8 collective-permute-done.1
  23.5 10.5 %collective-permute-start.2 = (bf16[4,1,32,256]{3,1,2,0:T(2,128)(2,1)S(1)}, bf16[4,1,32,256]{3,1,2,0:T(2,128)(2,1)S(1)}, u32[]{:S(2)}, u32[]{:S(2)}) collective-permute-start(bf16[4,1,32,256]{3,1,2,0:T(2,128)(2,1)S(1)} %get-tuple-element.106), channel_id=1, source_target_pairs={{0,4},{4,8},{8,12},{12,16},{16,20},{20,24},{24,28},{28,32},{32,36}... | collective-permute-start | bytes 196616 | tf_op jit(solution)/shard_map/ppermute | solution.py:17
  34.0 1.9 collective-permute-start.3
  35.9 4.1 collective-permute-done.2
  40.0 9.0 %collective-permute-done.3 = bf16[4,1,32,256]{3,1,2,0:T(2,128)(2,1)S(1)} collective-permute-done((bf16[4,1,32,256]{3,1,2,0:T(2,128)(2,1)S(1)}, bf16[4,1,32,256]{3,1,2,0:T(2,128)(2,1)S(1)}, u32[]{:S(2)}, u32[]{:S(2)}) %collective-permute-start.3) | collective-permute-done | bytes 65568 | tf_op jit(solution)/shard_map/ppermute | solution.py:19
  49.0 4.6 collective-permute-start.4
  53.7 1.3 collective-permute-start.5
  55.0 0.9 collective-permute-done.4
  55.9 6.5 %collective-permute-done.5 = bf16[4,18,1,256]{3,1,2,0:T(8,128)(2,1)S(1)} collective-permute-done((bf16[4,18,1,256]{3,1,2,0:T(8,128)(2,1)S(1)}, bf16[4,18,1,256]{3,1,2,0:T(8,128)(2,1)S(1)}, u32[]{:S(2)}, u32[]{:S(2)}) %collective-permute-start.5) | collective-permute-done | bytes 36896 | tf_op jit(solution)/shard_map/ppermute | solution.py:19
  62.4 1.1 maximum_bitcast_fusion
  63.5 0.6 copy.52
  64.1 0.7 pad.clone
  65.2 5.0 %fusion.24 = f32[2,16,8,5,256]{4,2,3,1,0:T(8,128)S(1)} fusion(bf16[3,3,3,256,256]{4,3,2,1,0:T(8,128)(2,1)S(1)} %copy-done, bf16[4,18,1,7,2,256]{5,3,4,1,0,2:T(8,128)(2,1)S(1)} %slice.56, bf16[4,18,1,8,5,256]{5,3,4,1,0,2:T(8,128)(2,1)S(1)} %copy.38, pred[8,5]{0,1:T(8,128)(4,1)S(1)} %copy-done.8), kind=kOutput, calls=%fused_computation.42 | convolution fusion | flops 4536369152 | bytes 6840360 | tf_op jit(solution)/shard_map/conv_general_dilated | solution.py:34
  71.3 0.5 copy.62
  71.9 1.2 reshape.155
  73.0 217.5 %all-gather.2.cloned.1.call-done = bf16[1024,16,3,128]{3,0,2,1:T(8,128)(2,1)} async-done(((bf16[1024,1,3,128]{3,0,2,1:T(8,128)(2,1)}), bf16[1024,16,3,128]{3,0,2,1:T(8,128)(2,1)}) %all-gather.2.cloned.1.call-update) | async-done | bytes 12582928 | tf_op jit(solution)/shard_map/all_gather | solution.py:49
  290.5 15.7 %copy.41 = bf16[1024,16,3,128]{0,3,2,1:T(8,128)(2,1)} copy(bf16[1024,16,3,128]{3,0,2,1:T(8,128)(2,1)} %all-gather.2.cloned.1.call-done) | data formatting | bytes 25165824 | tf_op jit(solution)/shard_map/all_gather | solution.py:49
  306.3 8.2 %convolution_convert_fusion = bf16[256,6144]{1,0:T(8,128)(2,1)S(1)} fusion(bf16[256,1024]{1,0:T(8,128)(2,1)} %reshape.155, bf16[1024,6144]{0,1:T(8,128)(2,1)} %bitcast.102), kind=kOutput, calls=%fused_computation.25 | convolution fusion | flops 3222798336 | bytes 16252928 | tf_op jit(solution)/shard_map/dot_general | solution.py:50
  314.5 0.5 copy.61
  315.0 76.1 %all_to_all.16 = bf16[256,16,384]{2,0,1:T(8,128)(2,1)S(1)} all-to-all(bf16[256,16,384]{2,0,1:T(8,128)(2,1)S(1)} %bitcast.105), channel_id=1, replica_groups=mesh['ta'=4,'ha'=16,'wa'=4] {'ta','wa'}, dimensions={1} | all-to-all | bytes 6291456 | tf_op jit(solution)/shard_map/all_to_all | solution.py:53
  391.1 3.9 reshape.157
  395.0 3.1 copy.43
  398.5 1.9 fusion.40
  400.4 8.9 %collective-permute-start.6 = (bf16[8,4,64,1,256]{4,2,1,0,3:T(8,128)(2,1)}, bf16[8,4,64,1,256]{4,2,1,0,3:T(8,128)(2,1)}, u32[]{:S(2)}, u32[]{:S(2)}) collective-permute-start(bf16[8,4,64,1,256]{4,2,1,0,3:T(8,128)(2,1)} %get-tuple-element.102), channel_id=1, source_target_pairs={{0,4},{4,8},{8,12},{12,16},{16,20},{20,24},{24,28},{28,32},{32,36}... | collective-permute-start | bytes 3145736 | tf_op jit(solution)/shard_map/ppermute | solution.py:17
  409.3 1.9 collective-permute-start.7
  411.3 1.0 copy.46
  412.2 1.3 slice_bitcast_fusion.1
  413.5 37.9 %collective-permute-done.6 = bf16[8,4,64,1,256]{4,2,1,0,3:T(8,128)(2,1)} collective-permute-done((bf16[8,4,64,1,256]{4,2,1,0,3:T(8,128)(2,1)}, bf16[8,4,64,1,256]{4,2,1,0,3:T(8,128)(2,1)}, u32[]{:S(2)}, u32[]{:S(2)}) %collective-permute-start.6) | collective-permute-done | bytes 1048608 | tf_op jit(solution)/shard_map/ppermute | solution.py:17
  451.4 5.2 %collective-permute-done.7 = bf16[8,4,64,1,256]{4,2,1,0,3:T(8,128)(2,1)} collective-permute-done((bf16[8,4,64,1,256]{4,2,1,0,3:T(8,128)(2,1)}, bf16[8,4,64,1,256]{4,2,1,0,3:T(8,128)(2,1)}, u32[]{:S(2)}, u32[]{:S(2)}) %collective-permute-start.7) | collective-permute-done | bytes 1048608 | tf_op jit(solution)/shard_map/ppermute | solution.py:19
  456.7 3.4 pad_maximum_fusion
  460.1 29.8 %while.12 = (s32[]{:T(128)}, bf16[2,8,4,64,1,128]{5,3,2,1,4,0:T(8,128)(2,1)}, s32[2]{0:T(128)S(1)}, bf16[8,16,64,1,256]{4,2,1,0,3:T(8,128)(2,1)}, s32[]{:T(128)}...) while((s32[]{:T(128)}, ...), condition=%wide.region_4.5_spmd, body=%wide.region_1.4_spmd.sunk | while | flops 824439104 | bytes 37807656 | solution.py:93
  460.1 0.6 dynamic_slice.28
  461.4 3.7 fusion.50
  465.1 3.4 fusion.51
  468.5 5.5 %fusion.52 = bf16[2,8,4,64,1,128]{5,3,2,1,4,0:T(8,128)(2,1)S(1)} fusion(bf16[2,8,4,64,1,128]{5,3,2,1,4,0:T(8,128)(2,1)S(1)} %copy-done.6, s32[]{:T(128)S(6)} %copy.66, f32[8,4,64,12,64]{2,4,3,1,0:T(8,128)S(1)} %get-tuple-element.153, f32[8,4,64]{2,1,0:T(4,128)S(1)} %fusion.51, f32[8,4,64]{2,1,0:T(4,128)S(1)} %get-tuple-element.154, ...), kind=kOutput, calls=%fused_computation.12.clone.1 | convolution fusion | flops 410779648 | bytes 14713356 | tf_op jit(solution)/shard_map/while/body/eval_jaxpr/thiajb,tjbhd->tiahd/dot_general | solution.py:88
  474.0 1.0 copy-done.7
  475.0 0.6 dynamic_slice.28
  476.3 3.7 fusion.50
  480.0 3.4 fusion.51
  483.4 5.5 %fusion.52 = bf16[2,8,4,64,1,128]{5,3,2,1,4,0:T(8,128)(2,1)S(1)} fusion(bf16[2,8,4,64,1,128]{5,3,2,1,4,0:T(8,128)(2,1)S(1)} %copy-done.6, s32[]{:T(128)S(6)} %copy.66, f32[8,4,64,12,64]{2,4,3,1,0:T(8,128)S(1)} %get-tuple-element.153, f32[8,4,64]{2,1,0:T(4,128)S(1)} %fusion.51, f32[8,4,64]{2,1,0:T(4,128)S(1)} %get-tuple-element.154, ...), kind=kOutput, calls=%fused_computation.12.clone.1 | convolution fusion | flops 410779648 | bytes 14713356 | tf_op jit(solution)/shard_map/while/body/eval_jaxpr/thiajb,tjbhd->tiahd/dot_general | solution.py:88
  488.9 1.0 copy-done.7
  489.9 2.4 copy.45
  (39 shorter events, 2.2 us)
Async XLA Ops:
  7.2 58.0 %copy-start = (bf16[3,3,3,256,256]{4,3,2,1,0:T(8,128)(2,1)S(1)}, bf16[3,3,3,256,256]{4,3,2,1,0:T(8,128)(2,1)}, u32[]{:S(2)}) copy-start(bf16[3,3,3,256,256]{4,3,2,1,0:T(8,128)(2,1)} %param.8) | copy-start | bytes 10616836
  7.2 283.3 %all-gather.2.cloned.1.call-start = ((), (), s32[]{:S(2)}) async-start(), calls=%async_computation.1 | async-start | bytes 13369344 | tf_op jit(solution)/shard_map/all_gather | solution.py:49
  11.2 8.2 %collective-permute-start = (bf16[1,16,32,256]{3,1,2,0:T(8,128)(2,1)S(1)}, bf16[1,16,32,256]{3,1,2,0:T(8,128)(2,1)S(1)}, u32[]{:S(2)}, u32[]{:S(2)}) collective-permute-start(bf16[1,16,32,256]{3,1,2,0:T(8,128)(2,1)S(1)} %get-tuple-element.108), channel_id=1, source_target_pairs={{0,64},{64,128},{128,192},{1,65},{65,129},{129,193},{2,66},{66,130... | collective-permute-start | bytes 786440 | tf_op jit(solution)/shard_map/ppermute | solution.py:17
  14.5 8.8 %collective-permute-start.1 = (bf16[1,16,32,256]{3,1,2,0:T(8,128)(2,1)S(1)}, bf16[1,16,32,256]{3,1,2,0:T(8,128)(2,1)S(1)}, u32[]{:S(2)}, u32[]{:S(2)}) collective-permute-start(bf16[1,16,32,256]{3,1,2,0:T(8,128)(2,1)S(1)} %get-tuple-element.109), channel_id=1, source_target_pairs={{64,0},{128,64},{192,128},{65,1},{129,65},{193,129},{66,2},{130,66... | collective-permute-start | bytes 786440 | tf_op jit(solution)/shard_map/ppermute | solution.py:19
  23.5 16.5 %collective-permute-start.2 = (bf16[4,1,32,256]{3,1,2,0:T(2,128)(2,1)S(1)}, bf16[4,1,32,256]{3,1,2,0:T(2,128)(2,1)S(1)}, u32[]{:S(2)}, u32[]{:S(2)}) collective-permute-start(bf16[4,1,32,256]{3,1,2,0:T(2,128)(2,1)S(1)} %get-tuple-element.106), channel_id=1, source_target_pairs={{0,4},{4,8},{8,12},{12,16},{16,20},{20,24},{24,28},{28,32},{32,36}... | collective-permute-start | bytes 196616 | tf_op jit(solution)/shard_map/ppermute | solution.py:17
  34.0 15.0 %collective-permute-start.3 = (bf16[4,1,32,256]{3,1,2,0:T(2,128)(2,1)S(1)}, bf16[4,1,32,256]{3,1,2,0:T(2,128)(2,1)S(1)}, u32[]{:S(2)}, u32[]{:S(2)}) collective-permute-start(bf16[4,1,32,256]{3,1,2,0:T(2,128)(2,1)S(1)} %get-tuple-element.107), channel_id=1, source_target_pairs={{4,0},{8,4},{12,8},{16,12},{20,16},{24,20},{28,24},{32,28},{36,32}... | collective-permute-start | bytes 196616 | tf_op jit(solution)/shard_map/ppermute | solution.py:19
  49.0 6.8 %collective-permute-start.4 = (bf16[4,18,1,256]{3,1,2,0:T(8,128)(2,1)S(1)}, bf16[4,18,1,256]{3,1,2,0:T(8,128)(2,1)S(1)}, u32[]{:S(2)}, u32[]{:S(2)}) collective-permute-start(bf16[4,18,1,256]{3,1,2,0:T(8,128)(2,1)S(1)} %get-tuple-element.104), channel_id=1, source_target_pairs={{0,1},{1,2},{2,3},{4,5},{5,6},{6,7},{8,9},{9,10},{10,11},{12,13},{... | collective-permute-start | bytes 110600 | tf_op jit(solution)/shard_map/ppermute | solution.py:17
  53.7 8.7 %collective-permute-start.5 = (bf16[4,18,1,256]{3,1,2,0:T(8,128)(2,1)S(1)}, bf16[4,18,1,256]{3,1,2,0:T(8,128)(2,1)S(1)}, u32[]{:S(2)}, u32[]{:S(2)}) collective-permute-start(bf16[4,18,1,256]{3,1,2,0:T(8,128)(2,1)S(1)} %get-tuple-element.105), channel_id=1, source_target_pairs={{1,0},{2,1},{3,2},{5,4},{6,5},{7,6},{9,8},{10,9},{11,10},{13,12},{... | collective-permute-start | bytes 110600 | tf_op jit(solution)/shard_map/ppermute | solution.py:19
  64.1 1.1 copy-start.8
  65.2 5.4 %copy-start.3 = (bf16[2,16,32,256]{3,2,1,0:T(8,128)(2,1)S(1)}, bf16[2,16,32,256]{3,2,1,0:T(8,128)(2,1)}, u32[]{:S(2)}) copy-start(bf16[2,16,32,256]{3,2,1,0:T(8,128)(2,1)} %param.6) | copy-start | bytes 1572868
  71.1 235.2 %copy-start.4 = (bf16[2,16,32,256]{3,1,2,0:T(8,128)(2,1)}, bf16[2,16,32,256]{3,1,2,0:T(8,128)(2,1)S(1)}, u32[]{:S(2)}) copy-start(bf16[2,16,32,256]{3,1,2,0:T(8,128)(2,1)S(1)} %fusion.35) | copy-start | bytes 1572868
  398.0 2.4 copy-start.2
  398.1 13.2 %copy-start.5 = (bf16[2,16,32,256]{3,1,2,0:T(8,128)(2,1)S(1)}, bf16[2,16,32,256]{3,1,2,0:T(8,128)(2,1)}, u32[]{:S(2)}) copy-start(bf16[2,16,32,256]{3,1,2,0:T(8,128)(2,1)} %copy-done.4) | copy-start | bytes 1572868
  400.4 51.0 %collective-permute-start.6 = (bf16[8,4,64,1,256]{4,2,1,0,3:T(8,128)(2,1)}, bf16[8,4,64,1,256]{4,2,1,0,3:T(8,128)(2,1)}, u32[]{:S(2)}, u32[]{:S(2)}) collective-permute-start(bf16[8,4,64,1,256]{4,2,1,0,3:T(8,128)(2,1)} %get-tuple-element.102), channel_id=1, source_target_pairs={{0,4},{4,8},{8,12},{12,16},{16,20},{20,24},{24,28},{28,32},{32,36}... | collective-permute-start | bytes 3145736 | tf_op jit(solution)/shard_map/ppermute | solution.py:17
  409.3 47.4 %collective-permute-start.7 = (bf16[8,4,64,1,256]{4,2,1,0,3:T(8,128)(2,1)}, bf16[8,4,64,1,256]{4,2,1,0,3:T(8,128)(2,1)}, u32[]{:S(2)}, u32[]{:S(2)}) collective-permute-start(bf16[8,4,64,1,256]{4,2,1,0,3:T(8,128)(2,1)} %get-tuple-element.103), channel_id=1, source_target_pairs={{4,0},{8,4},{12,8},{16,12},{20,16},{24,20},{28,24},{32,28},{36,32}... | collective-permute-start | bytes 3145736 | tf_op jit(solution)/shard_map/ppermute | solution.py:19
  465.1 3.5 copy-start.6
  474.0 1.0 copy-start.7
  479.9 3.5 copy-start.6
  488.9 1.0 copy-start.7
  489.9 2.4 copy-start.1
Sparse Core Ops, SparseCore 0:
  9.8 280.7 all-gather.1
where the time goes:
time: 500 us; the launch traced here: 499 us
  waiting for transfers between devices  289 us (58%)
  blocking collectives  76.1 us (15%)
  local copies, waits for them, and re-layouts  37.4 us (7%)
  starting transfers between devices  33.7 us (7%)
  matrix products  31.5 us (6%)
  other arithmetic  15.3 us (3%)
  between operations  14.3 us (3%)
    all_gather x1, waiting for transfers between devices, local(): every_head = lax.all_gather(qkv_weight, ('ta', 'wa'), axis=1, tiled=True)  218 us
    all_to_all x1, blocking collectives, local(): lax.all_to_all(projected, ('ta', 'wa'), split_axis=1, concat_axis=0, tile...  76.1 us
    ppermute x4, waiting for transfers between devices, extended(): lax.ppermute(tail, axis, [(i, (i + 1) % count) for i in range(ends)])  46.5 us
    ppermute x4, starting transfers between devices, extended(): lax.ppermute(tail, axis, [(i, (i + 1) % count) for i in range(ends)])  27.3 us
    ppermute x4, waiting for transfers between devices, extended(): lax.ppermute(head, axis, [((i + 1) % count, i) for i in range(ends)])  24.6 us
    all_gather x1, local copies, waits for them, and re-layouts, local(): every_head = lax.all_gather(qkv_weight, ('ta', 'wa'), axis=1, tiled=True)  15.7 us
    dot_general x2, matrix products, attend(): jnp.einsum('thiajb,tjbhd->tiahd', probs, value_part, preferred_element_ty...  10.9 us
  transfers between devices with their start and end apart: 9, of which 9 were waited for; matrix products, arithmetic and copies ran while one was open for 3% of the time, Pallas kernels for 0%

commit v1 on v0

--- a/solution.py
+++ b/solution.py
@@ -46,7 +46,10 @@
         .reshape(t_dev * rows_dev * cols_dev, 4 * channels)
     )
     width_in, head_dev, qkv_count, head_size = qkv_weight.shape
-    every_head = lax.all_gather(qkv_weight, ("ta", "wa"), axis=1, tiled=True)
+    every_head = jnp.concatenate(
+        lax.all_to_all(jnp.stack([qkv_weight] * lax.axis_size(("ta", "wa"))), ("ta", "wa"), 0, 0),
+        axis=1,
+    )
     projected = jnp.dot(
         patches, every_head.reshape(width_in, -1), preferred_element_type=jnp.float32
     ).astype(jnp.bfloat16)

time: 500 us -> 517 us (1.034)
  starting transfers between devices: 33.7 us -> 51.1 us
  between operations: 14.3 us -> 0.97 us
  matrix products: 31.5 us -> 42.7 us
  waiting for transfers between devices: 289 us -> 279 us
  blocking collectives: 76.1 us -> 85.7 us
    all_gather x1 -> x0, waiting for transfers between devices: 218 us -> none  [local(): every_head = lax.all_gather(qkv_weight, ('ta', 'wa'), axis=1, tiled=True)]
    ppermute x4, waiting for transfers between devices: 46.5 us -> 213 us  [extended(): lax.ppermute(tail, axis, [(i, (i + 1) % count) for i in range(ends)])]
    all_to_all x0 -> x1, waiting for transfers between devices: none -> 50.9 us  [local(): lax.all_to_all(jnp.stack([qkv_weight] * lax.axis_size(('ta', 'wa'))), ('t...]
    all_gather x1 -> x0, local copies, waits for them, and re-layouts: 15.7 us -> none  [local(): every_head = lax.all_gather(qkv_weight, ('ta', 'wa'), axis=1, tiled=True)]
    another operation x0 -> x2, local copies, waits for them, and re-layouts: none -> 9.68 us  [the longest x1 7.24 us: local(): jnp.stack([qkv_weight] * lax.axis_size(('ta', 'wa')))]
    all_to_all x1, blocking collectives: 76.1 us -> 85.7 us  [local(): lax.all_to_all(projected, ('ta', 'wa'), split_axis=1, concat_axis=0, tile...]
    while x8 -> x12, local copies, waits for them, and re-layouts: 1.94 us -> 11 us
    ppermute x4, waiting for transfers between devices: 24.6 us -> 15.8 us  [extended(): lax.ppermute(head, axis, [((i + 1) % count, i) for i in range(ends)])]
  transfers between devices with their start and end apart: 9 -> 9, of which waited for: 9 -> 8; matrix products, arithmetic and copies ran while one was open for 3% -> 3% of each run, Pallas kernels for 0% -> 0%
where the time goes in v1:
time: 517 us; the launch traced here: 516 us
  waiting for transfers between devices  279 us (54%)
  blocking collectives  85.7 us (17%)
  starting transfers between devices  51.1 us (10%)
  matrix products  42.7 us (8%)
  local copies, waits for them, and re-layouts  39.6 us (8%)
  other arithmetic  14.9 us (3%)
    ppermute x4, waiting for transfers between devices, extended(): lax.ppermute(tail, axis, [(i, (i + 1) % count) for i in range(ends)])  213 us
    all_to_all x1, blocking collectives, local(): lax.all_to_all(projected, ('ta', 'wa'), split_axis=1, concat_axis=0, tile...  85.7 us
    all_to_all x1, waiting for transfers between devices, local(): lax.all_to_all(jnp.stack([qkv_weight] * lax.axis_size(('ta', 'wa'))), ('t...  50.9 us
    ppermute x4, starting transfers between devices, extended(): lax.ppermute(tail, axis, [(i, (i + 1) % count) for i in range(ends)])  36 us
    dot_general x2, matrix products, attend(): jnp.einsum('thiajb,tjbhd->tiahd', probs, value_part, preferred_element_ty...  17.2 us
    ppermute x4, waiting for transfers between devices, extended(): lax.ppermute(head, axis, [((i + 1) % count, i) for i in range(ends)])  15.8 us
    dot_general x1, matrix products, local(): jnp.dot(patches, every_head.reshape(width_in, -1), preferred_element_type...  13.1 us
    while x12, local copies, waits for them, and re-layouts  11 us
  transfers between devices with their start and end apart: 9, of which 8 were waited for; matrix products, arithmetic and copies ran while one was open for 3% of the time, Pallas kernels for 0%

profile of v1, /device:TPU:3, one launch (start us, length us, event | category | flops | bytes accessed | tf_op | source)
XLA Modules:
  0.0 515.8 jit_solution(1629433801327672550)
XLA Ops:
  0.6 2.4 copy.42
  3.1 7.2 %stack.2 = bf16[16,1024,1,3,128]{1,4,3,2,0:T(8,128)(2,1)} broadcast(bf16[1024,3,128]{0,2,1:T(8,128)(2,1)} %copy.42), dimensions={1,3,4} | broadcast | bytes 13369344 | tf_op jit(solution)/shard_map/stack | solution.py:50
  10.3 8.5 %all-to-all-start = ((bf16[16,1024,1,3,128]{1,4,3,2,0:T(8,128)(2,1)}), bf16[16,1024,1,3,128]{1,4,3,2,0:T(8,128)(2,1)}, u32[]{:S(2)}, u32[]{:S(2)}) async-start(bf16[16,1024,1,3,128]{1,4,3,2,0:T(8,128)(2,1)} %stack.2), calls=%async_computation | async-start | bytes 25165824 | tf_op jit(solution)/shard_map/all_to_all | solution.py:50
  18.9 1.4 fusion.27
  20.3 1.5 fusion.34
  21.9 3.2 collective-permute-start
  25.1 1.3 collective-permute-start.1
  26.4 115.5 %collective-permute-done = bf16[1,16,32,256]{3,1,2,0:T(8,128)(2,1)S(1)} collective-permute-done((bf16[1,16,32,256]{3,1,2,0:T(8,128)(2,1)S(1)}, bf16[1,16,32,256]{3,1,2,0:T(8,128)(2,1)S(1)}, u32[]{:S(2)}, u32[]{:S(2)}) %collective-permute-start) | collective-permute-done | bytes 262176 | tf_op jit(solution)/shard_map/ppermute | solution.py:17
  141.9 2.9 collective-permute-done.1
  145.0 23.8 %collective-permute-start.2 = (bf16[4,1,32,256]{3,1,2,0:T(2,128)(2,1)S(1)}, bf16[4,1,32,256]{3,1,2,0:T(2,128)(2,1)S(1)}, u32[]{:S(2)}, u32[]{:S(2)}) collective-permute-start(bf16[4,1,32,256]{3,1,2,0:T(2,128)(2,1)S(1)} %get-tuple-element.106), channel_id=1, source_target_pairs={{0,4},{4,8},{8,12},{12,16},{16,20},{20,24},{24,28},{28,32},{32,36}... | collective-permute-start | bytes 196616 | tf_op jit(solution)/shard_map/ppermute | solution.py:17
  168.7 1.9 collective-permute-start.3
  170.7 56.9 %collective-permute-done.2 = bf16[4,1,32,256]{3,1,2,0:T(2,128)(2,1)S(1)} collective-permute-done((bf16[4,1,32,256]{3,1,2,0:T(2,128)(2,1)S(1)}, bf16[4,1,32,256]{3,1,2,0:T(2,128)(2,1)S(1)}, u32[]{:S(2)}, u32[]{:S(2)}) %collective-permute-start.2) | collective-permute-done | bytes 65568 | tf_op jit(solution)/shard_map/ppermute | solution.py:17
  227.6 5.8 %collective-permute-done.3 = bf16[4,1,32,256]{3,1,2,0:T(2,128)(2,1)S(1)} collective-permute-done((bf16[4,1,32,256]{3,1,2,0:T(2,128)(2,1)S(1)}, bf16[4,1,32,256]{3,1,2,0:T(2,128)(2,1)S(1)}, u32[]{:S(2)}, u32[]{:S(2)}) %collective-permute-start.3) | collective-permute-done | bytes 65568 | tf_op jit(solution)/shard_map/ppermute | solution.py:19
  233.4 1.3 collective-permute-start.4
  234.7 1.5 collective-permute-start.5
  236.2 3.3 collective-permute-done.5
  239.6 1.1 maximum_bitcast_fusion
  240.6 0.6 copy.54
  241.3 0.7 pad.clone
  242.4 5.0 fusion.24
  248.5 0.5 copy.64
  249.4 50.9 %all-to-all-done = bf16[16,1024,1,3,128]{1,4,3,2,0:T(8,128)(2,1)} async-done(((bf16[16,1024,1,3,128]{1,4,3,2,0:T(8,128)(2,1)}), bf16[16,1024,1,3,128]{1,4,3,2,0:T(8,128)(2,1)}, u32[]{:S(2)}, u32[]{:S(2)}) %all-to-all-start) | async-done | bytes 12582944 | tf_op jit(solution)/shard_map/all_to_all | solution.py:50
  300.3 13.1 %convolution_convert_fusion = bf16[256,6144]{1,0:T(8,128)(2,1)S(1)} fusion(bf16[256,1024]{1,0:T(8,128)(2,1)S(1)} %reshape.158, bf16[1024,6144]{0,1:T(8,128)(2,1)} %bitcast.24), kind=kOutput, calls=%fused_computation.25 | convolution fusion | flops 3222798336 | bytes 16252928 | tf_op jit(solution)/shard_map/dot_general | solution.py:53
  314.0 85.7 %all_to_all.21 = bf16[256,16,384]{2,0,1:T(8,128)(2,1)S(1)} all-to-all(bf16[256,16,384]{2,0,1:T(8,128)(2,1)S(1)} %bitcast.109), channel_id=1, replica_groups=mesh['ta'=4,'ha'=16,'wa'=4] {'ta','wa'}, dimensions={1} | all-to-all | bytes 6291456 | tf_op jit(solution)/shard_map/all_to_all | solution.py:56
  399.7 3.8 reshape.160
  403.5 3.1 copy.45
  407.1 1.9 fusion.40
  409.0 7.7 %collective-permute-start.6 = (bf16[8,4,64,1,256]{4,2,1,0,3:T(8,128)(2,1)}, bf16[8,4,64,1,256]{4,2,1,0,3:T(8,128)(2,1)}, u32[]{:S(2)}, u32[]{:S(2)}) collective-permute-start(bf16[8,4,64,1,256]{4,2,1,0,3:T(8,128)(2,1)} %get-tuple-element.102), channel_id=1, source_target_pairs={{0,4},{4,8},{8,12},{12,16},{16,20},{20,24},{24,28},{28,32},{32,36}... | collective-permute-start | bytes 3145736 | tf_op jit(solution)/shard_map/ppermute | solution.py:17
  416.7 1.9 collective-permute-start.7
  418.7 1.0 copy.48
  419.6 1.3 slice_bitcast_fusion.1
  420.9 40.2 %collective-permute-done.6 = bf16[8,4,64,1,256]{4,2,1,0,3:T(8,128)(2,1)} collective-permute-done((bf16[8,4,64,1,256]{4,2,1,0,3:T(8,128)(2,1)}, bf16[8,4,64,1,256]{4,2,1,0,3:T(8,128)(2,1)}, u32[]{:S(2)}, u32[]{:S(2)}) %collective-permute-start.6) | collective-permute-done | bytes 1048608 | tf_op jit(solution)/shard_map/ppermute | solution.py:17
  461.2 3.8 collective-permute-done.7
  465.0 3.4 pad_maximum_fusion
  468.3 45.0 %while.12 = (s32[]{:T(128)}, bf16[2,8,4,64,1,128]{5,3,2,1,4,0:T(8,128)(2,1)}, s32[2]{0:T(128)S(1)}, bf16[8,16,64,1,256]{4,2,1,0,3:T(8,128)(2,1)}, s32[]{:T(128)}...) while((s32[]{:T(128)}, ...), condition=%wide.region_4.5_spmd, body=%wide.region_1.4_spmd.sunk | while | flops 824439104 | bytes 62974008 | solution.py:96
  468.3 0.6 dynamic_slice.28
  469.6 3.7 fusion.50
  473.4 4.5 copy-done.2
  477.9 3.4 fusion.51
  481.3 8.6 %fusion.52 = bf16[2,8,4,64,1,128]{5,3,2,1,4,0:T(8,128)(2,1)S(1)} fusion(bf16[2,8,4,64,1,128]{5,3,2,1,4,0:T(8,128)(2,1)S(1)} %copy-done.7, s32[]{:T(128)} %get-tuple-element.167, f32[8,4,64,12,64]{2,4,3,1,0:T(8,128)} %copy-done.2, f32[8,4,64]{2,1,0:T(4,128)S(1)} %fusion.51, f32[8,4,64]{2,1,0:T(4,128)S(1)} %get-tuple-element.154, ...), kind=kOutput, calls=%fused_computation.12.clone.1 | convolution fusion | flops 410779648 | bytes 14713864 | tf_op jit(solution)/shard_map/while/body/eval_jaxpr/thiajb,tjbhd->tiahd/dot_general | solution.py:91
  489.9 1.0 copy-done.8
  490.9 0.6 dynamic_slice.28
  492.2 3.7 fusion.50
  495.9 4.5 copy-done.2
  500.4 3.4 fusion.51
  503.8 8.6 %fusion.52 = bf16[2,8,4,64,1,128]{5,3,2,1,4,0:T(8,128)(2,1)S(1)} fusion(bf16[2,8,4,64,1,128]{5,3,2,1,4,0:T(8,128)(2,1)S(1)} %copy-done.7, s32[]{:T(128)} %get-tuple-element.167, f32[8,4,64,12,64]{2,4,3,1,0:T(8,128)} %copy-done.2, f32[8,4,64]{2,1,0:T(4,128)S(1)} %fusion.51, f32[8,4,64]{2,1,0:T(4,128)S(1)} %get-tuple-element.154, ...), kind=kOutput, calls=%fused_computation.12.clone.1 | convolution fusion | flops 410779648 | bytes 14713864 | tf_op jit(solution)/shard_map/while/body/eval_jaxpr/thiajb,tjbhd->tiahd/dot_general | solution.py:91
  512.4 1.0 copy-done.8
  513.4 2.4 copy.47
  (45 shorter events, 3.1 us)
Async XLA Ops:
  0.6 241.7 %copy-start = (bf16[3,3,3,256,256]{4,3,2,1,0:T(8,128)(2,1)S(1)}, bf16[3,3,3,256,256]{4,3,2,1,0:T(8,128)(2,1)}, u32[]{:S(2)}) copy-start(bf16[3,3,3,256,256]{4,3,2,1,0:T(8,128)(2,1)} %param.8) | copy-start | bytes 10616836
  10.3 10.0 %copy-start.9 = (f32[256]{0:T(256)S(1)}, f32[256]{0:T(256)}, u32[]{:S(2)}) copy-start(f32[256]{0:T(256)} %param.7) | copy-start | bytes 3076
  10.3 290.0 %all-to-all-start = ((bf16[16,1024,1,3,128]{1,4,3,2,0:T(8,128)(2,1)}), bf16[16,1024,1,3,128]{1,4,3,2,0:T(8,128)(2,1)}, u32[]{:S(2)}, u32[]{:S(2)}) async-start(bf16[16,1024,1,3,128]{1,4,3,2,0:T(8,128)(2,1)} %stack.2), calls=%async_computation | async-start | bytes 25165824 | tf_op jit(solution)/shard_map/all_to_all | solution.py:50
  21.9 120.0 %collective-permute-start = (bf16[1,16,32,256]{3,1,2,0:T(8,128)(2,1)S(1)}, bf16[1,16,32,256]{3,1,2,0:T(8,128)(2,1)S(1)}, u32[]{:S(2)}, u32[]{:S(2)}) collective-permute-start(bf16[1,16,32,256]{3,1,2,0:T(8,128)(2,1)S(1)} %get-tuple-element.108), channel_id=1, source_target_pairs={{0,64},{64,128},{128,192},{1,65},{65,129},{129,193},{2,66},{66,130... | collective-permute-start | bytes 786440 | tf_op jit(solution)/shard_map/ppermute | solution.py:17
  25.1 119.6 %collective-permute-start.1 = (bf16[1,16,32,256]{3,1,2,0:T(8,128)(2,1)S(1)}, bf16[1,16,32,256]{3,1,2,0:T(8,128)(2,1)S(1)}, u32[]{:S(2)}, u32[]{:S(2)}) collective-permute-start(bf16[1,16,32,256]{3,1,2,0:T(8,128)(2,1)S(1)} %get-tuple-element.109), channel_id=1, source_target_pairs={{64,0},{128,64},{192,128},{65,1},{129,65},{193,129},{66,2},{130,66... | collective-permute-start | bytes 786440 | tf_op jit(solution)/shard_map/ppermute | solution.py:19
  145.0 82.6 %collective-permute-start.2 = (bf16[4,1,32,256]{3,1,2,0:T(2,128)(2,1)S(1)}, bf16[4,1,32,256]{3,1,2,0:T(2,128)(2,1)S(1)}, u32[]{:S(2)}, u32[]{:S(2)}) collective-permute-start(bf16[4,1,32,256]{3,1,2,0:T(2,128)(2,1)S(1)} %get-tuple-element.106), channel_id=1, source_target_pairs={{0,4},{4,8},{8,12},{12,16},{16,20},{20,24},{24,28},{28,32},{32,36}... | collective-permute-start | bytes 196616 | tf_op jit(solution)/shard_map/ppermute | solution.py:17
  168.7 64.6 %collective-permute-start.3 = (bf16[4,1,32,256]{3,1,2,0:T(2,128)(2,1)S(1)}, bf16[4,1,32,256]{3,1,2,0:T(2,128)(2,1)S(1)}, u32[]{:S(2)}, u32[]{:S(2)}) collective-permute-start(bf16[4,1,32,256]{3,1,2,0:T(2,128)(2,1)S(1)} %get-tuple-element.107), channel_id=1, source_target_pairs={{4,0},{8,4},{12,8},{16,12},{20,16},{24,20},{28,24},{32,28},{36,32}... | collective-permute-start | bytes 196616 | tf_op jit(solution)/shard_map/ppermute | solution.py:19
  233.4 2.8 collective-permute-start.4
  234.7 4.8 collective-permute-start.5
  241.3 1.1 copy-start.10
  242.4 5.4 %copy-start.4 = (bf16[2,16,32,256]{3,2,1,0:T(8,128)(2,1)S(1)}, bf16[2,16,32,256]{3,2,1,0:T(8,128)(2,1)}, u32[]{:S(2)}) copy-start(bf16[2,16,32,256]{3,2,1,0:T(8,128)(2,1)} %param.6) | copy-start | bytes 1572868
  248.3 65.2 %copy-start.5 = (bf16[2,16,32,256]{3,1,2,0:T(8,128)(2,1)}, bf16[2,16,32,256]{3,1,2,0:T(8,128)(2,1)S(1)}, u32[]{:S(2)}) copy-start(bf16[2,16,32,256]{3,1,2,0:T(8,128)(2,1)S(1)} %fusion.35) | copy-start | bytes 1572868
  406.6 2.4 copy-start.3
  406.6 12.0 %copy-start.6 = (bf16[2,16,32,256]{3,1,2,0:T(8,128)(2,1)S(1)}, bf16[2,16,32,256]{3,1,2,0:T(8,128)(2,1)}, u32[]{:S(2)}) copy-start(bf16[2,16,32,256]{3,1,2,0:T(8,128)(2,1)} %copy-done.5) | copy-start | bytes 1572868
  409.0 52.2 %collective-permute-start.6 = (bf16[8,4,64,1,256]{4,2,1,0,3:T(8,128)(2,1)}, bf16[8,4,64,1,256]{4,2,1,0,3:T(8,128)(2,1)}, u32[]{:S(2)}, u32[]{:S(2)}) collective-permute-start(bf16[8,4,64,1,256]{4,2,1,0,3:T(8,128)(2,1)} %get-tuple-element.102), channel_id=1, source_target_pairs={{0,4},{4,8},{8,12},{12,16},{16,20},{20,24},{24,28},{28,32},{32,36}... | collective-permute-start | bytes 3145736 | tf_op jit(solution)/shard_map/ppermute | solution.py:17
  416.7 48.3 %collective-permute-start.7 = (bf16[8,4,64,1,256]{4,2,1,0,3:T(8,128)(2,1)}, bf16[8,4,64,1,256]{4,2,1,0,3:T(8,128)(2,1)}, u32[]{:S(2)}, u32[]{:S(2)}) collective-permute-start(bf16[8,4,64,1,256]{4,2,1,0,3:T(8,128)(2,1)} %get-tuple-element.103), channel_id=1, source_target_pairs={{4,0},{8,4},{12,8},{16,12},{20,16},{24,20},{28,24},{32,28},{36,32}... | collective-permute-start | bytes 3145736 | tf_op jit(solution)/shard_map/ppermute | solution.py:19
  473.3 4.5 copy-start.2
  477.9 3.4 copy-start.7
  489.9 1.0 copy-start.8
  495.9 4.5 copy-start.2
  500.4 3.4 copy-start.7
  512.4 1.0 copy-start.8
  513.4 2.4 copy-start.1
